TPU v7x, 32 devices: a whole 2x2x4 slice. The times are simulated.
32 devices in a mesh: row: 8 (over z, x), col: 4 (over y, core).
Axes of the slice: x: 2, y: 2, z: 4, core: 2. Of those that a mesh axis runs over, the one named last changes fastest.
Arguments:
- vectors: bfloat16 [4, 4, 8, 16, 256], P(None, 'col', 'row'), may hold values from -6 to 6
- tiles: bfloat16 [8, 4, 64, 256, 256], P('row', 'col'), may hold values from -0.0625 to 0.0625
- tile_coords: int32 [8, 4, 64, 2], P('row', 'col'), may hold values from 0 to 127, as said below
- tile_count: int32 [8, 4], P('row', 'col'), may hold values from 16 to 64, as said below
Outputs:
- product: float32 [4, 4, 8, 16, 256], P(None, 'col', 'row')
Inputs may be any that keep to these rules, and one draw needn't show every extreme that they name: `tile_coords`: for the device in grid row r and grid column c every slot's block row I has I % 8 == r, its block column J has (J // 8) % 4 == c, and J <= I. `tile_count`: counts differ from device to device; in every draw some device uses all 64 slots and some other uses 64 // 4.
All inputs are finite; a program needn't handle non-finite values.
Results may differ from a plain program's by a relative error of at most 0.0003.
Values may be sent and summed in bfloat16 or wider, within the bound.
No kernel may reach another device: no remote copies, remote signals or barrier semaphores. Data moves between devices by JAX's collectives and lax.ppermute only.
A program may use at most 64 MiB of HBM per device.

v0:
```python
import jax
import jax.numpy as jnp
from jax import lax
from jax.sharding import PartitionSpec as P

TILE_GROUP = 8


def body(vectors, tiles, tile_coords, tile_count):
    grid_rows = lax.axis_size("row")
    grid_cols = lax.axis_size("col")
    repeats = vectors.shape[0]
    vec_count = vectors.shape[3]
    tile_width = vectors.shape[4]
    slot_count = tiles.shape[2]
    cells = grid_rows * grid_cols
    local_blocks = vectors.reshape(repeats, 1, vec_count, tile_width)
    column_blocks = lax.all_gather(local_blocks, "row", axis=1, tiled=True).reshape(
        repeats * grid_rows, vec_count, tile_width
    )
    row_blocks = lax.all_gather(local_blocks, "col", axis=1, tiled=True).reshape(
        repeats * grid_cols, vec_count, tile_width
    )
    matrices_all = tiles.reshape(slot_count, tile_width, tile_width)
    coords_all = tile_coords.reshape(slot_count, 2)
    filled = tile_count.reshape(())
    turns = (filled + TILE_GROUP - 1) // TILE_GROUP
    row_slots = jnp.arange(repeats * grid_cols, dtype=jnp.int32)
    col_slots = jnp.arange(repeats * grid_rows, dtype=jnp.int32)
    group_ids = jnp.arange(TILE_GROUP, dtype=jnp.int32)

    def load_group(turn):
        start = turn * TILE_GROUP
        matrices = lax.dynamic_slice_in_dim(matrices_all, start, TILE_GROUP, 0)
        positions = lax.dynamic_slice_in_dim(coords_all, start, TILE_GROUP, 0)
        active = start + group_ids < filled
        upper_index = positions[:, 0] // cells * grid_cols + positions[:, 0] % cells // grid_rows
        lower_index = positions[:, 1] // cells * grid_rows + positions[:, 1] % grid_rows
        row_hits = jnp.where(
            active[:, None] & (upper_index[:, None] == row_slots[None, :]), 1.0, 0.0
        ).astype(jnp.float32)
        col_hits = jnp.where(
            active[:, None] & (lower_index[:, None] == col_slots[None, :]), 1.0, 0.0
        ).astype(jnp.float32)
        return (matrices, upper_index, lower_index, row_hits, col_hits)

    def forward_add(total, matrices, lower_index, row_hits):
        sources = jnp.take(column_blocks, lower_index, axis=0)
        terms = jnp.einsum("snb,smb->snm", sources, matrices, preferred_element_type=jnp.float32)
        return total + jnp.einsum("su,snm->unm", row_hits, terms, precision=lax.Precision.HIGHEST)

    def mirror_add(total, matrices, upper_index, col_hits):
        targets = jnp.take(row_blocks, upper_index, axis=0)
        terms = jnp.einsum("snb,sbm->snm", targets, matrices, preferred_element_type=jnp.float32)
        return total + jnp.einsum("sv,snm->vnm", col_hits, terms, precision=lax.Precision.HIGHEST)

    row_start = jnp.zeros((repeats * grid_cols, vec_count, tile_width), jnp.float32)
    col_start = jnp.zeros((repeats * grid_rows, vec_count, tile_width), jnp.float32)

    def forward_turn(turn, total):
        matrices, upper_index, lower_index, row_hits, col_hits = load_group(turn)
        return forward_add(total, matrices, lower_index, row_hits)

    def mirror_turn(turn, total):
        matrices, upper_index, lower_index, row_hits, col_hits = load_group(turn)
        return mirror_add(total, matrices, upper_index, col_hits)

    row_acc = lax.fori_loop(0, turns, forward_turn, row_start)
    col_acc = lax.fori_loop(0, turns, mirror_turn, col_start)
    row_terms = row_acc.reshape(repeats, grid_cols, vec_count, tile_width)
    col_terms = col_acc.reshape(repeats, grid_rows, vec_count, tile_width)
    row_whole = lax.psum(row_terms, "col")
    col_whole = lax.psum(col_terms, "row")
    row_mine = lax.dynamic_slice_in_dim(row_whole, lax.axis_index("col"), 1, 1)
    col_mine = lax.dynamic_slice_in_dim(col_whole, lax.axis_index("row"), 1, 1)
    return (row_mine + col_mine).reshape(repeats, 1, 1, vec_count, tile_width)


def solution(mesh):
    return jax.shard_map(
        body,
        mesh=mesh,
        in_specs=(
            P(None, "col", "row", None, None),
            P("row", "col", None, None, None),
            P("row", "col", None, None),
            P("row", "col"),
        ),
        out_specs=P(None, "col", "row", None, None),
        check_vma=False,
    )
```

profile of v0, /device:TPU:0, one launch (start us, length us, event | category | flops | bytes accessed | tf_op | source)
XLA Modules:
  0.0 193.9 jit_solution(9262916242494318244)
XLA Ops:
  7.2 32.8 %all-gather = bf16[4,8,1,16,256]{4,3,2,1,0:T(8,128)(2,1)S(1)} all-gather(bf16[4,1,1,16,256]{4,3,2,1,0:T(8,128)(2,1)} %param.8), channel_id=2, replica_groups=mesh['row'=8,'col'=4] {'row'}, dimensions={1}, use_global_device_ids=true | all-gather | bytes 294912 | tf_op jit(solution)/shard_map/all_gather | solution.py:18
  40.0 16.9 %while.30 = (s32[]{:T(128)}, f32[16,16,256]{2,0,1:T(8,128)S(1)}, s32[]{:T(128)}, s32[]{:T(128)}, s32[64,2]{0,1:T(2,128)}, /*index=5*/bf16[32,16,256]{2,1,0:T(8,1...) while((s32[]{:T(128)}, f32[16,16,256]{2,0,1:T(8,128)S(1)}, ...), condition=%wide.region_1.2_spmd.clone, body=%wide.region_0.1_spmd.clone.sunk | while | flops 23168940 | bytes 2036267 | solution.py:68
  40.0 0.8 constant_dynamic-slice_fusion.4
  41.4 1.6 fusion.66
  44.3 0.8 constant_dynamic-slice_fusion.4
  45.6 1.6 fusion.66
  49.8 1.6 fusion.66
  54.0 1.6 fusion.66
  56.9 0.9 copy.5
  57.8 15.6 %all-gather.1 = bf16[4,4,1,16,256]{4,3,2,1,0:T(8,128)(2,1)S(1)} all-gather(bf16[4,1,1,16,256]{4,3,2,1,0:T(8,128)(2,1)S(1)} %copy-done), channel_id=3, replica_groups=mesh['row'=8,'col'=4] {'col'}, dimensions={1}, use_global_device_ids=true | all-gather | bytes 163840 | tf_op jit(solution)/shard_map/all_gather | solution.py:21
  73.5 17.5 %while.31 = (s32[]{:T(128)}, f32[32,16,256]{2,0,1:T(8,128)S(1)}, s32[]{:T(128)}, s32[]{:T(128)}, s32[64,2]{0,1:T(2,128)}, /*index=5*/bf16[16,16,256]{2,1,0:T(8,1...) while((s32[]{:T(128)}, f32[32,16,256]{2,0,1:T(8,128)S(1)}, ...), condition=%wide.region_4.5_spmd.clone, body=%wide.region_3.4_spmd.clone.sunk | while | flops 29526316 | bytes 2560555 | solution.py:69
  74.8 1.5 fusion.72
  77.0 0.8 convolution_add_fusion.5
  79.2 1.5 fusion.72
  81.4 0.8 convolution_add_fusion.5
  82.2 0.8 constant_dynamic-slice_fusion.5
  83.6 1.5 fusion.72
  85.8 0.8 convolution_add_fusion.5
  88.0 1.5 fusion.72
  90.2 0.8 convolution_add_fusion.5
  91.0 1.1 copy.6
  92.1 11.5 %all-reduce.3.cloned.1.call-done = f32[4,4,16,256]{3,2,1,0:T(8,128)} async-done(((f32[4,4,16,256]{3,2,1,0:T(8,128)}), f32[4,4,16,256]{3,2,1,0:T(8,128)}) %all-reduce.3.cloned.1.call-update) | async-done | bytes 262160 | tf_op jit(solution)/shard_map/psum | solution.py:72
  103.6 82.0 %all-reduce.5.cloned.1.call-done = f32[4,8,16,256]{3,2,1,0:T(8,128)} async-done(((f32[4,8,16,256]{3,2,1,0:T(8,128)}), f32[4,8,16,256]{3,2,1,0:T(8,128)}) %all-reduce.5.cloned.1.call-update) | async-done | bytes 524304 | tf_op jit(solution)/shard_map/psum | solution.py:73
  185.6 1.5 add_bitcast_fusion.1
  (57 shorter events, 16.1 us)
Async XLA Ops:
  6.5 51.3 %copy-start = (bf16[4,1,1,16,256]{4,3,2,1,0:T(8,128)(2,1)S(1)}, bf16[4,1,1,16,256]{4,3,2,1,0:T(8,128)(2,1)}, u32[]{:S(2)}) copy-start(bf16[4,1,1,16,256]{4,3,2,1,0:T(8,128)(2,1)} %param.8) | copy-start | bytes 98308
  6.5 97.1 %all-reduce.3.cloned.1.call-start = ((), (), s32[]{:S(2)}) async-start(), calls=%async_computation | async-start | bytes 524288 | tf_op jit(solution)/shard_map/psum | solution.py:72
  57.8 127.8 %all-reduce.5.cloned.1.call-start = ((), (), s32[]{:S(2)}) async-start(), calls=%async_computation.1 | async-start | bytes 1048576 | tf_op jit(solution)/shard_map/psum | solution.py:73
Sparse Core Ops, SparseCore 0:
  57.9 45.6 all-reduce.2
  107.0 78.5 all-reduce.4
where the time goes:
time: 195 us; the launch traced here: 194 us
  waiting for transfers between devices  93.5 us (48%)
  blocking collectives  48.3 us (25%)
  matrix products  17.8 us (9%)
  between operations  14.1 us (7%)
  local copies, waits for them, and re-layouts  12.5 us (6%)
  other arithmetic  7.16 us (4%)
    psum x1, waiting for transfers between devices, body(): col_whole = lax.psum(col_terms, 'row')  82 us
    all_gather x1, blocking collectives, body(): lax.all_gather(local_blocks, 'row', axis=1, tiled=True)  32.8 us
    all_gather x1, blocking collectives, body(): lax.all_gather(local_blocks, 'col', axis=1, tiled=True)  15.6 us
    psum x1, waiting for transfers between devices, body(): row_whole = lax.psum(row_terms, 'col')  11.5 us
    dot_general x4, matrix products, forward_add(): jnp.einsum('snb,smb->snm', sources, matrices, preferred_element_type=jnp....  6.44 us
    dot_general x4, matrix products, mirror_add(): jnp.einsum('snb,sbm->snm', targets, matrices, preferred_element_type=jnp....  6.05 us
    dynamic_slice x8, local copies, waits for them, and re-layouts, load_group(): positions = lax.dynamic_slice_in_dim(coords_all, start, TILE_GROUP, 0)  6.04 us
    lt x8, other arithmetic, load_group(): active = start + group_ids < filled  5.23 us
  transfers between devices with their start and end apart: 2, of which 2 were waited for; matrix products, arithmetic and copies ran while one was open for 9% of the time, Pallas kernels for 0%

commit v1 on v0

--- a/solution.py
+++ b/solution.py
@@ -4,6 +4,12 @@
 from jax.sharding import PartitionSpec as P
 
 TILE_GROUP = 8
+
+
+def gather_from_all(x, axis, dim):
+    devices = lax.axis_size(axis)
+    repeats = [devices if d == dim else 1 for d in range(x.ndim)]
+    return lax.all_to_all(jnp.tile(x, repeats), axis, split_axis=dim, concat_axis=dim, tiled=True)
 
 
 def body(vectors, tiles, tile_coords, tile_count):
@@ -15,7 +21,7 @@
     slot_count = tiles.shape[2]
     cells = grid_rows * grid_cols
     local_blocks = vectors.reshape(repeats, 1, vec_count, tile_width)
-    column_blocks = lax.all_gather(local_blocks, "row", axis=1, tiled=True).reshape(
+    column_blocks = gather_from_all(local_blocks, "row", 1).reshape(
         repeats * grid_rows, vec_count, tile_width
     )
     row_blocks = lax.all_gather(local_blocks, "col", axis=1, tiled=True).reshape(

time: 195 us -> 174 us (0.89)
  blocking collectives: 48.3 us -> 5.63 us
  waiting for transfers between devices: 93.5 us -> 106 us
  starting transfers between devices: 0.04 us -> 7.36 us
    all_gather x1 -> x0, blocking collectives: 32.8 us -> none  [body(): lax.all_gather(local_blocks, 'row', axis=1, tiled=True)]
    psum x1, waiting for transfers between devices: 11.5 us -> 33.8 us  [body(): row_whole = lax.psum(row_terms, 'col')]
    all_gather x1, blocking collectives: 15.6 us -> 5.63 us  [body(): lax.all_gather(local_blocks, 'col', axis=1, tiled=True)]
    psum x1, waiting for transfers between devices: 82 us -> 72 us  [body(): col_whole = lax.psum(col_terms, 'row')]
    all_to_all x0 -> x1, starting transfers between devices: none -> 7.28 us  [gather_from_all(): lax.all_to_all(jnp.tile(x, repeats), axis, split_axis=dim, concat_axis=di...]
  transfers between devices with their start and end apart: 2 -> 3, of which waited for: 2 -> 2; matrix products, arithmetic and copies ran while one was open for 9% -> 21% of each run, Pallas kernels for 0% -> 0%
where the time goes in v1:
time: 174 us; the launch traced here: 172 us
  waiting for transfers between devices  106 us (61%)
  matrix products  17.8 us (10%)
  between operations  14.1 us (8%)
  local copies, waits for them, and re-layouts  14 us (8%)
  starting transfers between devices  7.36 us (4%)
  other arithmetic  7.16 us (4%)
  blocking collectives  5.63 us (3%)
    psum x1, waiting for transfers between devices, body(): col_whole = lax.psum(col_terms, 'row')  72 us
    psum x1, waiting for transfers between devices, body(): row_whole = lax.psum(row_terms, 'col')  33.8 us
    all_to_all x1, starting transfers between devices, gather_from_all(): lax.all_to_all(jnp.tile(x, repeats), axis, split_axis=dim, concat_axis=di...  7.28 us
    dot_general x4, matrix products, forward_add(): jnp.einsum('snb,smb->snm', sources, matrices, preferred_element_type=jnp....  6.44 us
    dot_general x4, matrix products, mirror_add(): jnp.einsum('snb,sbm->snm', targets, matrices, preferred_element_type=jnp....  6.04 us
    dynamic_slice x8, local copies, waits for them, and re-layouts, load_group(): positions = lax.dynamic_slice_in_dim(coords_all, start, TILE_GROUP, 0)  6.04 us
    all_gather x1, blocking collectives, body(): lax.all_gather(local_blocks, 'col', axis=1, tiled=True)  5.63 us
    lt x8, other arithmetic, load_group(): active = start + group_ids < filled  5.23 us
  transfers between devices with their start and end apart: 3, of which 2 were waited for; matrix products, arithmetic and copies ran while one was open for 21% of the time, Pallas kernels for 0%

profile of v1, /device:TPU:0, one launch (start us, length us, event | category | flops | bytes accessed | tf_op | source)
XLA Modules:
  0.0 172.4 jit_solution(2892209236763014326)
XLA Ops:
  6.5 1.5 tile.9
  8.0 7.3 %all-to-all-start = ((bf16[4,8,16,256]{3,2,0,1:T(8,128)(2,1)}), bf16[4,8,16,256]{3,2,0,1:T(8,128)(2,1)S(1)}, u32[]{:S(2)}, u32[]{:S(2)}) async-start(bf16[4,8,16,256]{3,2,0,1:T(8,128)(2,1)} %tile.9), calls=%async_computation | async-start | bytes 524288 | tf_op jit(solution)/shard_map/all_to_all | solution.py:12
  16.0 5.6 %all-gather = bf16[4,4,1,16,256]{4,3,2,1,0:T(8,128)(2,1)S(1)} all-gather(bf16[4,1,1,16,256]{4,3,2,1,0:T(8,128)(2,1)} %param.8), channel_id=2, replica_groups=mesh['row'=8,'col'=4] {'col'}, dimensions={1}, use_global_device_ids=true | all-gather | bytes 163840 | tf_op jit(solution)/shard_map/all_gather | solution.py:27
  21.7 17.5 %while.31 = (s32[]{:T(128)}, f32[32,16,256]{2,0,1:T(8,128)S(1)}, s32[]{:T(128)}, s32[]{:T(128)}, s32[64,2]{0,1:T(2,128)}, /*index=5*/bf16[16,16,256]{2,1,0:T(8,1...) while((s32[]{:T(128)}, f32[32,16,256]{2,0,1:T(8,128)S(1)}, ...), condition=%wide.region_4.5_spmd.clone, body=%wide.region_3.4_spmd.clone.sunk | while | flops 29526316 | bytes 2560555 | solution.py:75
  21.7 0.8 constant_dynamic-slice_fusion.5
  23.1 1.5 fusion.72
  25.3 0.8 convolution_add_fusion.5
  26.1 0.8 constant_dynamic-slice_fusion.5
  27.4 1.5 fusion.72
  29.6 0.8 convolution_add_fusion.5
  31.8 1.5 fusion.72
  34.0 0.8 convolution_add_fusion.5
  36.2 1.5 fusion.72
  38.4 0.8 convolution_add_fusion.5
  39.2 1.1 copy.17
  40.4 16.9 %while.30 = (s32[]{:T(128)}, f32[16,16,256]{2,0,1:T(8,128)S(1)}, s32[]{:T(128)}, s32[]{:T(128)}, s32[64,2]{0,1:T(2,128)}, /*index=5*/bf16[32,16,256]{2,1,0:T(8,1...) while((s32[]{:T(128)}, f32[16,16,256]{2,0,1:T(8,128)S(1)}, ...), condition=%wide.region_1.2_spmd.clone, body=%wide.region_0.1_spmd.clone.sunk | while | flops 23168940 | bytes 2036267 | solution.py:74
  41.8 1.6 fusion.66
  46.0 1.6 fusion.66
  50.2 1.6 fusion.66
  54.4 1.6 fusion.66
  57.3 0.9 copy.16
  58.2 72.0 %all-reduce.5.cloned.1.call-done = f32[4,8,16,256]{3,2,1,0:T(8,128)} async-done(((f32[4,8,16,256]{3,2,1,0:T(8,128)}), f32[4,8,16,256]{3,2,1,0:T(8,128)}) %all-reduce.5.cloned.1.call-update) | async-done | bytes 524304 | tf_op jit(solution)/shard_map/psum | solution.py:79
  130.2 33.8 %all-reduce.3.cloned.1.call-done = f32[4,4,16,256]{3,2,1,0:T(8,128)} async-done(((f32[4,4,16,256]{3,2,1,0:T(8,128)}), f32[4,4,16,256]{3,2,1,0:T(8,128)}) %all-reduce.3.cloned.1.call-update) | async-done | bytes 262160 | tf_op jit(solution)/shard_map/psum | solution.py:78
  164.1 1.5 add_bitcast_fusion.1
  (58 shorter events, 16.9 us)
Async XLA Ops:
  8.0 32.3 %all-to-all-start = ((bf16[4,8,16,256]{3,2,0,1:T(8,128)(2,1)}), bf16[4,8,16,256]{3,2,0,1:T(8,128)(2,1)S(1)}, u32[]{:S(2)}, u32[]{:S(2)}) async-start(bf16[4,8,16,256]{3,2,0,1:T(8,128)(2,1)} %tile.9), calls=%async_computation | async-start | bytes 524288 | tf_op jit(solution)/shard_map/all_to_all | solution.py:12
  15.3 114.9 %all-reduce.5.cloned.1.call-start = ((), (), s32[]{:S(2)}) async-start(), calls=%async_computation.2 | async-start | bytes 1048576 | tf_op jit(solution)/shard_map/psum | solution.py:79
  40.3 123.8 %all-reduce.3.cloned.1.call-start = ((), (), s32[]{:S(2)}) async-start(), calls=%async_computation.1 | async-start | bytes 524288 | tf_op jit(solution)/shard_map/psum | solution.py:78
Sparse Core Ops, SparseCore 0:
  40.4 89.7 all-reduce.4
  132.5 31.4 all-reduce.2
